TPU v7x, 128 devices: a whole 4x4x4 slice. The times are simulated.
128 devices in a mesh: seq: 16 (over z_hi, y, core), head: 8 (over x, z_lo).
Axes of the slice: x: 4, y: 4, z: 4 (z_hi: 2, z_lo: 2; z = z_hi * 2 + z_lo), core: 2. Of those that a mesh axis runs over, the one named last changes fastest.
Arguments:
- queries: bfloat16 [128, 16384], P(None, 'head')
- cache_keys: bfloat16 [2, 65536, 1024], P(None, 'seq', 'head'), may hold values from -6 to 6
- cache_values: bfloat16 [2, 65536, 1024], P(None, 'seq', 'head'), may hold values from -6 to 6
- tree_keys: bfloat16 [128, 1024], P(None, 'head')
- tree_values: bfloat16 [128, 1024], P(None, 'head'), may hold values from -6 to 6
- ancestors: int32 [2, 64, 64], replicated, may hold values from 0 to 1, as said below
- filled_extents: int32 [2], replicated, may hold values from 1 to 65536, as said below
- out_weight: bfloat16 [16384, 16384], P('head', 'seq'), may hold values from -0.046875 to 0.046875
- residual: bfloat16 [128, 16384], P(None, 'seq'), may hold values from -6 to 6
- norm_gain: bfloat16 [16384], replicated, may hold values from 0.099609375 to 1.8984375
- vocab_weight: bfloat16 [16384, 65536], P(None, ('seq', 'head'))
- candidates: int32 [128], replicated, may hold values from 0 to 65535
- amateur: float32 [128], replicated, may hold values from -12 to -1
Outputs:
- hidden: bfloat16 [128, 16384], P(None, ('seq', 'head'))
- contrast: float32 [128], replicated
Inputs may be any that keep to these rules, and one draw needn't show every extreme that they name: Rows are nodes; node 0 is the root; every node's parent has a smaller index; ancestors[b, i, i] = 1. Positions 0 to filled_extents[b] - 1 of request b are live; some request has length 65536.
All inputs are finite; a program needn't handle non-finite values.
Results may differ from a plain program's by a relative error of at most 0.006.
Values may be sent and summed in bfloat16 or wider, within the bound.
No kernel may reach another device: no remote copies, remote signals or barrier semaphores. Data moves between devices by JAX's collectives and lax.ppermute only.
A program may use at most 192 MiB of HBM per device.

v0:
```python
import jax
import jax.numpy as jnp
from jax import lax
from jax.sharding import PartitionSpec as P

NODES_REQ = 64
D = 16384
HD = 128
NEG_FILL = -1e30
EPSILON = 1e-05


def joined(x, axis, join):
    gathered = jax.tree.map(
        lambda a, kind: lax.all_gather(a.astype(kind), axis),
        x,
        (jnp.bfloat16, jnp.bfloat16, jnp.bfloat16),
    )

    def take(source):
        return jax.tree.map(
            lambda a, own: lax.dynamic_index_in_dim(a, source, 0, False).astype(own.dtype),
            gathered,
            x,
        )

    return lax.fori_loop(
        1, lax.axis_size(axis), lambda source, state: join(state, take(source)), take(0)
    )


def joined_2(part, axis, combine):
    gathered = jax.tree.map(lambda a: lax.all_gather(a, axis), part)

    def take(source):
        return jax.tree.map(lambda a: lax.dynamic_index_in_dim(a, source, 0, False), gathered)

    return lax.fori_loop(
        1, lax.axis_size(axis), lambda source, state: combine(state, take(source)), take(0)
    )


def blend(former, latter):
    highest = jnp.maximum(former[0], latter[0])
    factor_a = jnp.exp(former[0] - highest)
    factor_b = jnp.exp(latter[0] - highest)
    return (
        highest,
        former[1] * factor_a + latter[1] * factor_b,
        former[2] * factor_a[..., None] + latter[2] * factor_b[..., None],
    )


def join_vocab(former, latter):
    highest = jnp.maximum(former[0], latter[0])
    total = former[1] * jnp.exp(former[0] - highest) + latter[1] * jnp.exp(latter[0] - highest)
    return (highest, total, former[2] + latter[2])


def body(
    queries,
    cache_keys,
    cache_values,
    tree_keys,
    tree_values,
    ancestors,
    filled_extents,
    out_weight,
    residual,
    norm_gain,
    vocab_weight,
    candidates,
    amateur,
):
    requests, element_locations, kv_width = cache_keys.shape
    kv_local = kv_width // HD
    heads_local = queries.shape[1] // HD
    group_size = heads_local // kv_local
    score_scale = HD ** (-0.5)
    grouped = queries.reshape(requests, NODES_REQ, kv_local, group_size, HD)
    stored_lookup_entries = cache_keys.reshape(requests, element_locations, kv_local, HD)
    stored_content_entries = cache_values.reshape(requests, element_locations, kv_local, HD)
    insertion_start_index = lax.axis_index("seq") * element_locations
    entry_validity = (insertion_start_index + jnp.arange(element_locations, dtype=jnp.int32))[
        None, :
    ] < filled_extents[:, None]
    joint_visibility_filter = entry_validity[:, None, None, None, :]
    scores = (
        jnp.einsum(
            "bnkgd,bpkd->bkgnp", grouped, stored_lookup_entries, preferred_element_type=jnp.float32
        )
        * score_scale
    )
    scores = jnp.where(joint_visibility_filter, scores, NEG_FILL)
    local_max = scores.max(-1)
    guessed_branch_lookups = tree_keys.reshape(requests, NODES_REQ, kv_local, HD)
    guessed_branch_contents = tree_values.reshape(requests, NODES_REQ, kv_local, HD)
    tree_live = (ancestors > 0)[:, None, None, :, :]
    tree_scores = (
        jnp.einsum(
            "bnkgd,bjkd->bkgnj", grouped, guessed_branch_lookups, preferred_element_type=jnp.float32
        )
        * score_scale
    )
    tree_scores = jnp.where(tree_live, tree_scores, NEG_FILL)
    tree_max = tree_scores.max(-1)
    tree_weights = jnp.where(tree_live, jnp.exp(tree_scores - tree_max[..., None]), 0.0)
    tree_sum = tree_weights.sum(-1)
    tree_summed = jnp.einsum(
        "bkgnj,bjkd->bkgnd",
        tree_weights.astype(jnp.bfloat16),
        guessed_branch_contents,
        preferred_element_type=jnp.float32,
    )
    weights = jnp.where(joint_visibility_filter, jnp.exp(scores - local_max[..., None]), 0.0)
    weight_sum = weights.sum(-1)
    summed = jnp.einsum(
        "bkgnp,bpkd->bkgnd",
        weights.astype(jnp.bfloat16),
        stored_content_entries,
        preferred_element_type=jnp.float32,
    )
    highest, weight_sum, summed = joined((local_max, weight_sum, summed), "seq", blend)
    highest, weight_sum, summed = blend(
        (highest, weight_sum, summed), (tree_max, tree_sum, tree_summed)
    )
    attended = (
        (summed / weight_sum[..., None])
        .transpose(0, 3, 1, 2, 4)
        .reshape(requests * NODES_REQ, heads_local * HD)
        .astype(jnp.bfloat16)
    )
    projected = jnp.dot(attended, out_weight, preferred_element_type=jnp.float32)
    cols_seq = out_weight.shape[1]
    share_width = cols_seq // lax.axis_size("head")
    vocab_local = vocab_weight.shape[1]
    share = lax.psum_scatter(
        projected.astype(jnp.bfloat16), "head", scatter_dimension=1, tiled=True
    ).astype(jnp.float32)
    residual_part = lax.dynamic_slice_in_dim(
        residual, lax.axis_index("head") * share_width, share_width, 1
    )
    hidden = (residual_part.astype(jnp.float32) + share).astype(jnp.bfloat16)
    hidden_f = hidden.astype(jnp.float32)
    squares = lax.psum(jnp.sum(hidden_f * hidden_f, axis=1), ("seq", "head"))
    gain_cols = lax.dynamic_slice_in_dim(
        norm_gain, lax.axis_index(("seq", "head")) * share_width, share_width, 0
    )
    normed = (
        hidden_f * lax.rsqrt(squares / D + EPSILON)[:, None] * gain_cols.astype(jnp.float32)
    ).astype(jnp.bfloat16)
    logits = jnp.dot(
        lax.all_gather(normed, ("seq", "head"), axis=1, tiled=True),
        vocab_weight,
        preferred_element_type=jnp.float32,
    )
    vocab_start = lax.axis_index(("seq", "head")) * vocab_local
    peak_logit = logits.max(axis=1)
    mass_sum = jnp.sum(jnp.exp(logits - peak_logit[:, None]), axis=1)
    matches = jnp.arange(vocab_local, dtype=jnp.int32)[None, :] + vocab_start == candidates[:, None]
    chosen = jnp.sum(jnp.where(matches, logits, 0.0), axis=1)
    peak_logit, mass_sum, chosen = joined_2(
        (peak_logit, mass_sum, chosen), ("seq", "head"), join_vocab
    )
    contrast = chosen - (peak_logit + jnp.log(mass_sum)) - amateur
    return (hidden, contrast)


def solution(mesh):
    in_specs = (
        P(None, "head"),
        P(None, "seq", "head"),
        P(None, "seq", "head"),
        P(None, "head"),
        P(None, "head"),
        P(),
        P(),
        P("head", "seq"),
        P(None, "seq"),
        P(),
        P(None, ("seq", "head")),
        P(),
        P(),
    )
    out_specs = (P(None, ("seq", "head")), P())
    return jax.shard_map(body, mesh=mesh, in_specs=in_specs, out_specs=out_specs, check_vma=False)
```

profile of v0, /device:TPU:0, one launch (start us, length us, event | category | flops | bytes accessed | tf_op | source)
XLA Modules:
  0.0 1467.3 jit_solution(13490291166868993872)
XLA Ops:
  7.2 0.0 copy-start
  7.2 0.0 all-gather.14.cloned.1.call-start
  7.2 1.3 copy.49
  8.5 0.7 broadcast_compare_fusion.1
  9.3 0.0 copy-done
  9.3 0.0 copy-start.7
  9.3 13.6 bitcast_reduce_fusion
  22.9 0.0 copy-done.7
  22.9 14.7 %fusion.29 = bf16[2,16,64,128]{3,2,1,0:T(8,128)(2,1)} fusion(bf16[2,4096,128]{2,1,0:T(8,128)(2,1)S(1)} %copy-done.7, f32[2,4096,64,16]{1,2,3,0:T(8,128)} %get-tuple-element.428, f32[2,16,64]{2,1,0:T(8,128)S(1)} %get-tuple-element.427, pred[2,4096]{1,0:T(4,128)(4,1)S(1)} %broadcast_compare_fusion.1), kind=kOutput, calls=%fused_computation.41 | convolution fusion | flops 2189688832 | bytes 36192256 | tf_op jit(solution)/shard_map/bkgnp,bpkd->bkgnd/dot_general | solution.py:117
  37.6 0.0 all-gather.14.cloned.1.call-update
  37.7 0.0 reduce-scatter.4.cloned.1.call-start
  37.7 0.0 copy-done.3
  37.8 0.1 copy.37
  37.9 25.8 %all-gather = bf16[32,16,64]{2,1,0:T(8,128)(2,1)S(1)} all-gather(bf16[2,16,64]{2,1,0:T(8,128)(2,1)S(1)} %convert_element_type.176), channel_id=2, replica_groups=mesh['seq'=16,'head'=8] {'seq'}, dimensions={0}, use_global_device_ids=true | all-gather | bytes 69632 | tf_op jit(solution)/shard_map/all_gather | solution.py:15
  63.7 16.1 %fusion.15 = bf16[2,16,64]{2,1,0:T(8,128)(2,1)S(1)} fusion(f32[2,4096,64,16]{1,2,3,0:T(8,128)} %get-tuple-element.428, f32[2,16,64]{2,1,0:T(8,128)S(1)} %get-tuple-element.427, pred[2,4096]{1,0:T(4,128)(4,1)S(1)} %broadcast_compare_fusion.1), kind=kLoop, calls=%fused_computation.26 | loop fusion | flops 41940992 | bytes 33574912 | tf_op jit(solution)/shard_map/reduce_sum | solution.py:116
  79.8 19.8 %all-gather.1 = bf16[32,16,64]{2,1,0:T(8,128)(2,1)S(1)} all-gather(bf16[2,16,64]{2,1,0:T(8,128)(2,1)S(1)} %fusion.15), channel_id=3, replica_groups=mesh['seq'=16,'head'=8] {'seq'}, dimensions={0}, use_global_device_ids=true | all-gather | bytes 69632 | tf_op jit(solution)/shard_map/all_gather | solution.py:15
  99.6 0.0 copy-done.4
  99.6 0.6 fusion.64
  100.2 0.2 fusion.36
  100.5 13.1 all-gather.14.cloned.1.call-done
  113.6 1.1 fusion.42
  114.7 31.3 %while.38 = (s32[]{:T(128)}, f32[2,1,16,64]{3,2,1,0:T(8,128)S(1)}, f32[2,1,16,64]{3,2,1,0:T(8,128)S(1)}, f32[2,1,16,64,128]{4,3,2,1,0:T(8,128)S(1)}, bf16[16,2,1...) while((s32[]{:T(128)}, f32[2,1,16,64]{3,2,1,0:T(8,128)S(1)}, ...), condition=%wide.region_3.4_spmd, body=%wide.region_2.3_spmd.sunk | while | flops 1069061 | bytes 2732187 | solution.py:27
  114.8 2.0 fusion.77
  116.9 2.0 fusion.77
  119.0 2.0 fusion.77
  121.1 2.0 fusion.77
  123.2 2.0 fusion.77
  125.3 2.0 fusion.77
  127.3 2.0 fusion.77
  129.4 2.0 fusion.77
  131.5 2.0 fusion.77
  133.6 2.0 fusion.77
  135.7 2.0 fusion.77
  137.8 2.0 fusion.77
  139.9 2.0 fusion.77
  142.0 2.0 fusion.77
  144.0 2.0 fusion.77
  146.1 0.0 copy-done.8
  146.1 1.2 fusion.35
  147.3 0.3 copy.41
  147.6 0.0 copy-start.1
  147.6 0.0 copy-start.5
  147.7 0.0 copy-start.6
  147.7 3.0 convolution_convert_fusion
  150.7 0.8 copy.47
  151.6 0.0 reduce-scatter.4.cloned.1.call-update
  151.6 0.2 all-gather.12.cloned.1.call-start
  151.8 0.8 dynamic-slice_convert_fusion
  152.6 34.4 %reduce-scatter.4.cloned.1.call-done = bf16[128,128]{1,0:T(8,128)(2,1)} async-done(((bf16[1024,128]{1,0:T(8,128)(2,1)}), bf16[128,128]{1,0:T(8,128)(2,1)}) %reduce-scatter.4.cloned.1.call-update) | async-done | bytes 32784
  187.0 0.9 copy.48
  187.9 0.9 fusion.48
  188.8 0.0 copy-start.2
  188.8 62.8 %psum.7 = f32[128]{0:T(128)S(1)} all-reduce(f32[128]{0:T(128)S(1)} %get-tuple-element.419), channel_id=1, replica_groups=mesh['seq'=16,'head'=8] {'seq','head'}, use_global_device_ids=true, to_apply=%region_8.9 | all-reduce | flops 128 | bytes 1024 | tf_op jit(solution)/shard_map/psum | solution.py:145
  251.6 0.7 fusion.50
  252.3 0.0 all-gather.12.cloned.1.call-update
  252.3 255.9 %all-gather.12.cloned.1.call-done = bf16[128,16384]{1,0:T(8,128)(2,1)} async-done(((bf16[128,128]{1,0:T(8,128)(2,1)}), bf16[128,16384]{1,0:T(8,128)(2,1)}) %all-gather.12.cloned.1.call-update) | async-done | bytes 4194320 | tf_op jit(solution)/shard_map/all_gather | solution.py:153
  508.2 9.5 fusion.65
  517.7 313.6 %all-gather.6 = f32[128,1,128]{2,1,0:T(1,128)S(1)} all-gather(f32[1,1,128]{2,1,0:T(1,128)S(1)} %bitcast.225), channel_id=5, replica_groups=mesh['seq'=16,'head'=8] {'seq','head'}, dimensions={0}, use_global_device_ids=true | all-gather | bytes 66048 | tf_op jit(solution)/shard_map/all_gather | solution.py:33
  831.3 0.0 copy-done.5
  831.3 0.2 select_reduce_fusion
  831.5 310.2 %all-gather.7 = f32[128,1,128]{2,1,0:T(1,128)S(1)} all-gather(f32[1,1,128]{2,1,0:T(1,128)S(1)} %bitcast.227), channel_id=6, replica_groups=mesh['seq'=16,'head'=8] {'seq','head'}, dimensions={0}, use_global_device_ids=true | all-gather | bytes 66048 | tf_op jit(solution)/shard_map/all_gather | solution.py:33
  1141.8 312.4 %all-gather.8 = f32[128,1,128]{2,1,0:T(1,128)S(1)} all-gather(f32[1,1,128]{2,1,0:T(1,128)S(1)} %bitcast.226), channel_id=7, replica_groups=mesh['seq'=16,'head'=8] {'seq','head'}, dimensions={0}, use_global_device_ids=true | all-gather | bytes 66048 | tf_op jit(solution)/shard_map/all_gather | solution.py:33
  1454.2 6.0 while.39
  1460.2 0.5 subtract_subtract_fusion
  (189 shorter events, 4.3 us)
Async XLA Ops:
  7.2 2.1 copy-start
  7.2 106.4 %all-gather.14.cloned.1.call-start = ((), (), s32[]{:S(2)}) async-start(), calls=%async_computation.2 | async-start | bytes 8912896 | tf_op jit(solution)/shard_map/all_gather | solution.py:15
  9.3 13.6 copy-start.7
  22.9 14.8 %copy-start.3 = (s32[2,64,64]{2,1,0:T(8,128)S(1)}, s32[2,64,64]{2,1,0:T(8,128)}, u32[]{:S(2)}) copy-start(s32[2,64,64]{2,1,0:T(8,128)} %param.22) | copy-start | bytes 98308
  37.7 149.4 %reduce-scatter.4.cloned.1.call-start = ((), (), s32[]{:S(2)}) async-start(), calls=%async_computation.3 | async-start | bytes 294912
  63.7 35.9 %copy-start.4 = (bf16[128,128]{1,0:T(8,128)(2,1)S(1)}, bf16[128,128]{1,0:T(8,128)(2,1)}, u32[]{:S(2)}) copy-start(bf16[128,128]{1,0:T(8,128)(2,1)} %param.20) | copy-start | bytes 98308
  79.8 66.3 %copy-start.8 = (bf16[128,128]{1,0:T(8,128)(2,1)S(1)}, bf16[128,128]{1,0:T(8,128)(2,1)}, u32[]{:S(2)}) copy-start(bf16[128,128]{1,0:T(8,128)(2,1)} %param.21) | copy-start | bytes 98308
  147.6 1313.1 %copy-start.1 = (bf16[2,4096,128]{2,1,0:T(8,128)(2,1)S(1)}, bf16[2,4096,128]{2,1,0:T(8,128)(2,1)}, u32[]{:S(2)}) copy-start(bf16[2,4096,128]{2,1,0:T(8,128)(2,1)} %param.18) | copy-start | bytes 6291460
  147.6 683.7 %copy-start.5 = (s32[128]{0:T(128)S(1)}, s32[128]{0:T(128)}, u32[]{:S(2)}) copy-start(s32[128]{0:T(128)} %param.28) | copy-start | bytes 1540
  147.7 1312.5 %copy-start.6 = (f32[128]{0:T(128)S(1)}, f32[128]{0:T(128)}, u32[]{:S(2)}) copy-start(f32[128]{0:T(128)} %param.29) | copy-start | bytes 1540
  151.6 356.7 %all-gather.12.cloned.1.call-start = ((), (), s32[]{:S(2)}) async-start(), calls=%async_computation.1 | async-start | bytes 4227072 | tf_op jit(solution)/shard_map/all_gather | solution.py:153
  188.8 1272.0 %copy-start.2 = (bf16[128,128]{1,0:T(8,128)(2,1)}, bf16[128,128]{1,0:T(8,128)(2,1)S(1)}, u32[]{:S(2)}) copy-start(bf16[128,128]{1,0:T(8,128)(2,1)S(1)} %get-tuple-element.420) | copy-start | bytes 98308
Sparse Core Ops, SparseCore 0:
  37.8 75.7 all-gather.13
  151.7 35.2 reduce-scatter.3
  252.4 255.7 all-gather.11
where the time goes:
time: 1470 us
  blocking collectives  1040 us (71%)
  waiting for transfers between devices  303 us (21%)
  other arithmetic  55.5 us (4%)
  matrix products  42.7 us (3%)
    all_gather x3, blocking collectives, joined_2(): gathered = jax.tree.map(lambda a: lax.all_gather(a, axis), part)  936 us
    all_gather x1, waiting for transfers between devices, body(): lax.all_gather(normed, ('seq', 'head'), axis=1, tiled=True)  256 us
    psum x1, blocking collectives, body(): squares = lax.psum(jnp.sum(hidden_f * hidden_f, axis=1), ('seq', 'head'))  62.8 us
    all_gather x2, blocking collectives, joined(): lax.all_gather(a.astype(kind), axis)  45.6 us
    unnamed x4, waiting for transfers between devices  34.5 us
    add x15, other arithmetic, blend(): former[2] * factor_a[..., None] + latter[2] * factor_b[..., None]  30 us
  transfers between devices with their start and end apart: 3, of which 3 were waited for; matrix products, arithmetic and copies ran while one was open for 1% of the time, Pallas kernels for 0%

commit v1 on v0

--- a/solution.py
+++ b/solution.py
@@ -142,7 +142,9 @@
     )
     hidden = (residual_part.astype(jnp.float32) + share).astype(jnp.bfloat16)
     hidden_f = hidden.astype(jnp.float32)
-    squares = lax.psum(jnp.sum(hidden_f * hidden_f, axis=1), ("seq", "head"))
+    own_2 = jnp.sum(hidden_f * hidden_f, axis=1)
+    pieces = lax.all_gather(own_2, ("seq", "head"))
+    squares = jnp.sum(pieces, axis=0)
     gain_cols = lax.dynamic_slice_in_dim(
         norm_gain, lax.axis_index(("seq", "head")) * share_width, share_width, 0
     )

time: 1470 us -> 1710 us (1.16)
  blocking collectives: 1040 us -> 1290 us
    all_gather x0 -> x1, blocking collectives: none -> 310 us  [body(): pieces = lax.all_gather(own_2, ('seq', 'head'))]
    psum x1 -> x0, blocking collectives: 62.8 us -> none  [body(): squares = lax.psum(jnp.sum(hidden_f * hidden_f, axis=1), ('seq', 'head'))]
where the time goes in v1:
time: 1710 us
  blocking collectives  1290 us (75%)
  waiting for transfers between devices  301 us (18%)
  other arithmetic  55.6 us (3%)
  matrix products  42.7 us (2%)
    all_gather x3, blocking collectives, joined_2(): gathered = jax.tree.map(lambda a: lax.all_gather(a, axis), part)  936 us
    all_gather x1, blocking collectives, body(): pieces = lax.all_gather(own_2, ('seq', 'head'))  310 us
    all_gather x1, waiting for transfers between devices, body(): lax.all_gather(normed, ('seq', 'head'), axis=1, tiled=True)  254 us
    all_gather x2, blocking collectives, joined(): lax.all_gather(a.astype(kind), axis)  45.6 us
    unnamed x4, waiting for transfers between devices  34.5 us
  transfers between devices with their start and end apart: 3, of which 3 were waited for; matrix products, arithmetic and copies ran while one was open for 1% of the time, Pallas kernels for 0%

profile of v1, /device:TPU:0, one launch (start us, length us, event | category | flops | bytes accessed | tf_op | source)
XLA Modules:
  0.0 1712.8 jit_solution(8684733451749384064)
XLA Ops:
  7.2 0.0 copy-start
  7.2 0.0 all-gather.16.cloned.1.call-start
  7.2 1.3 copy.49
  8.5 0.7 broadcast_compare_fusion.1
  9.3 0.0 copy-done
  9.3 0.0 copy-start.7
  9.3 13.6 bitcast_reduce_fusion
  22.9 0.0 copy-done.7
  22.9 14.7 fusion.29
  37.6 0.0 all-gather.16.cloned.1.call-update
  37.7 0.0 reduce-scatter.4.cloned.1.call-start
  37.7 0.0 copy-done.3
  37.8 0.1 copy.37
  37.9 25.8 %all-gather = bf16[32,16,64]{2,1,0:T(8,128)(2,1)S(1)} all-gather(bf16[2,16,64]{2,1,0:T(8,128)(2,1)S(1)} %convert_element_type.176), channel_id=2, replica_groups=mesh['seq'=16,'head'=8] {'seq'}, dimensions={0}, use_global_device_ids=true | all-gather | bytes 69632 | tf_op jit(solution)/shard_map/all_gather | solution.py:15
  63.7 16.1 fusion.15
  79.8 19.8 %all-gather.1 = bf16[32,16,64]{2,1,0:T(8,128)(2,1)S(1)} all-gather(bf16[2,16,64]{2,1,0:T(8,128)(2,1)S(1)} %fusion.15), channel_id=3, replica_groups=mesh['seq'=16,'head'=8] {'seq'}, dimensions={0}, use_global_device_ids=true | all-gather | bytes 69632 | tf_op jit(solution)/shard_map/all_gather | solution.py:15
  99.6 0.0 copy-done.4
  99.6 0.6 fusion.64
  100.2 0.2 fusion.36
  100.5 13.1 all-gather.16.cloned.1.call-done
  113.6 1.1 fusion.42
  114.7 31.3 %while.38 = (s32[]{:T(128)}, f32[2,1,16,64]{3,2,1,0:T(8,128)S(1)}, f32[2,1,16,64]{3,2,1,0:T(8,128)S(1)}, f32[2,1,16,64,128]{4,3,2,1,0:T(8,128)S(1)}, bf16[16,2,1...) while((s32[]{:T(128)}, f32[2,1,16,64]{3,2,1,0:T(8,128)S(1)}, ...), condition=%wide.region_3.4_spmd, body=%wide.region_2.3_spmd.sunk | while | flops 1069061 | bytes 2732187 | solution.py:27
  114.8 2.0 fusion.77
  116.9 2.0 fusion.77
  119.0 2.0 fusion.77
  121.1 2.0 fusion.77
  123.2 2.0 fusion.77
  125.3 2.0 fusion.77
  127.3 2.0 fusion.77
  129.4 2.0 fusion.77
  131.5 2.0 fusion.77
  133.6 2.0 fusion.77
  135.7 2.0 fusion.77
  137.8 2.0 fusion.77
  139.9 2.0 fusion.77
  142.0 2.0 fusion.77
  144.0 2.0 fusion.77
  146.1 1.2 fusion.35
  147.3 0.3 copy.41
  147.6 0.0 copy-start.1
  147.6 0.0 copy-start.5
  147.7 0.0 copy-start.6
  147.7 3.0 convolution_convert_fusion
  150.7 0.8 copy.47
  151.6 0.0 reduce-scatter.4.cloned.1.call-update
  151.6 0.2 all-gather.14.cloned.1.call-start
  151.8 0.8 dynamic-slice_convert_fusion
  152.6 34.4 %reduce-scatter.4.cloned.1.call-done = bf16[128,128]{1,0:T(8,128)(2,1)} async-done(((bf16[1024,128]{1,0:T(8,128)(2,1)}), bf16[128,128]{1,0:T(8,128)(2,1)}) %reduce-scatter.4.cloned.1.call-update) | async-done | bytes 32784
  187.0 0.9 copy.48
  187.9 0.9 fusion.48
  188.8 0.0 copy-start.2
  188.8 310.2 %all-gather.7 = f32[128,1,128]{2,1,0:T(1,128)S(1)} all-gather(f32[1,1,128]{2,1,0:T(1,128)S(1)} %bitcast.229), channel_id=5, replica_groups=mesh['seq'=16,'head'=8] {'seq','head'}, dimensions={0}, use_global_device_ids=true | all-gather | bytes 66048 | tf_op jit(solution)/shard_map/all_gather | solution.py:146
  499.0 0.2 reduce_sum.60
  499.2 0.7 fusion.50
  499.8 0.0 all-gather.14.cloned.1.call-update
  499.9 253.8 %all-gather.14.cloned.1.call-done = bf16[128,16384]{1,0:T(8,128)(2,1)} async-done(((bf16[128,128]{1,0:T(8,128)(2,1)}), bf16[128,16384]{1,0:T(8,128)(2,1)}) %all-gather.14.cloned.1.call-update) | async-done | bytes 4194320 | tf_op jit(solution)/shard_map/all_gather | solution.py:155
  753.7 9.5 fusion.65
  763.2 313.6 %all-gather.8 = f32[128,1,128]{2,1,0:T(1,128)S(1)} all-gather(f32[1,1,128]{2,1,0:T(1,128)S(1)} %bitcast.226), channel_id=6, replica_groups=mesh['seq'=16,'head'=8] {'seq','head'}, dimensions={0}, use_global_device_ids=true | all-gather | bytes 66048 | tf_op jit(solution)/shard_map/all_gather | solution.py:33
  1076.8 0.2 select_reduce_fusion
  1077.0 310.2 %all-gather.9 = f32[128,1,128]{2,1,0:T(1,128)S(1)} all-gather(f32[1,1,128]{2,1,0:T(1,128)S(1)} %bitcast.228), channel_id=7, replica_groups=mesh['seq'=16,'head'=8] {'seq','head'}, dimensions={0}, use_global_device_ids=true | all-gather | bytes 66048 | tf_op jit(solution)/shard_map/all_gather | solution.py:33
  1387.2 312.4 %all-gather.10 = f32[128,1,128]{2,1,0:T(1,128)S(1)} all-gather(f32[1,1,128]{2,1,0:T(1,128)S(1)} %bitcast.227), channel_id=8, replica_groups=mesh['seq'=16,'head'=8] {'seq','head'}, dimensions={0}, use_global_device_ids=true | all-gather | bytes 66048 | tf_op jit(solution)/shard_map/all_gather | solution.py:33
  1699.7 6.1 while.39
  1705.7 0.5 subtract_subtract_fusion
  1706.3 0.0 copy-done.1
  (190 shorter events, 4.3 us)
Async XLA Ops:
  7.2 2.1 copy-start
  7.2 106.4 %all-gather.16.cloned.1.call-start = ((), (), s32[]{:S(2)}) async-start(), calls=%async_computation.2 | async-start | bytes 8912896 | tf_op jit(solution)/shard_map/all_gather | solution.py:15
  9.3 13.6 copy-start.7
  22.9 14.8 copy-start.3
  37.7 149.4 %reduce-scatter.4.cloned.1.call-start = ((), (), s32[]{:S(2)}) async-start(), calls=%async_computation.3 | async-start | bytes 294912
  63.7 35.9 %copy-start.4 = (bf16[128,128]{1,0:T(8,128)(2,1)S(1)}, bf16[128,128]{1,0:T(8,128)(2,1)}, u32[]{:S(2)}) copy-start(bf16[128,128]{1,0:T(8,128)(2,1)} %param.20) | copy-start | bytes 98308
  79.8 66.3 %copy-start.8 = (bf16[128,128]{1,0:T(8,128)(2,1)S(1)}, bf16[128,128]{1,0:T(8,128)(2,1)}, u32[]{:S(2)}) copy-start(bf16[128,128]{1,0:T(8,128)(2,1)} %param.21) | copy-start | bytes 98308
  147.6 1558.6 %copy-start.1 = (bf16[2,4096,128]{2,1,0:T(8,128)(2,1)S(1)}, bf16[2,4096,128]{2,1,0:T(8,128)(2,1)}, u32[]{:S(2)}) copy-start(bf16[2,4096,128]{2,1,0:T(8,128)(2,1)} %param.18) | copy-start | bytes 6291460
  147.6 929.2 %copy-start.5 = (s32[128]{0:T(128)S(1)}, s32[128]{0:T(128)}, u32[]{:S(2)}) copy-start(s32[128]{0:T(128)} %param.28) | copy-start | bytes 1540
  147.7 1558.1 %copy-start.6 = (f32[128]{0:T(128)S(1)}, f32[128]{0:T(128)}, u32[]{:S(2)}) copy-start(f32[128]{0:T(128)} %param.29) | copy-start | bytes 1540
  151.6 602.1 %all-gather.14.cloned.1.call-start = ((), (), s32[]{:S(2)}) async-start(), calls=%async_computation.1 | async-start | bytes 4227072 | tf_op jit(solution)/shard_map/all_gather | solution.py:155
  188.8 1517.5 %copy-start.2 = (bf16[128,128]{1,0:T(8,128)(2,1)}, bf16[128,128]{1,0:T(8,128)(2,1)S(1)}, u32[]{:S(2)}) copy-start(bf16[128,128]{1,0:T(8,128)(2,1)S(1)} %get-tuple-element.420) | copy-start | bytes 98308
Sparse Core Ops, SparseCore 0:
  37.8 75.7 all-gather.15
  151.7 35.2 reduce-scatter.3
  500.0 253.6 all-gather.13
